TPU v7x, 256 devices: a whole 4x4x8 slice. The times are simulated.
256 devices in a mesh: grp: 4 (over y), seq: 16 (over z, core), head: 4 (over x).
Axes of the slice: x: 4, y: 4, z: 8, core: 2. Of those that a mesh axis runs over, the one named last changes fastest.
Arguments:
- keys: bfloat16 [32, 8192, 1536], P('grp', 'seq', 'head'), may hold values from -6 to 6
- values: bfloat16 [32, 8192, 1536], P('grp', 'seq', 'head'), may hold values from -6 to 6
- log_forget: float32 [32, 24, 8192], P('grp', 'head', 'seq'), may hold values from -0.6 to 0, as said below
- keep: int32 [32, 8192], P('grp', 'seq'), may hold values from 0 to 1, as said below
- merge_weight: float32 [32, 8192], P('grp', 'seq'), may hold values from 0.1 to 10
- lengths: int32 [32], P('grp'), may hold values from 64 to 8192, as said below
- route: int32 [32], P('grp'), may hold values from 0 to 31, as said below
- fresh: bfloat16 [3, 32, 1536], P(None, 'grp', 'head'), may hold values from -7.5 to 7.5
- new_forget: bfloat16 [32, 24], P('grp', 'head'), may hold values from -1 to -0.049804688
- out_weight: bfloat16 [1536, 1536], P('head', 'seq'), may hold values from -0.15625 to 0.15625
Outputs:
- compact_keys: bfloat16 [32, 4096, 1536], P('grp', 'seq', 'head')
- compact_values: bfloat16 [32, 4096, 1536], P('grp', 'seq', 'head')
- compact_decay: float32 [32, 24, 4096], P('grp', 'head', 'seq')
- layer_out: bfloat16 [32, 1536], P('grp', 'seq')
Inputs may be any that keep to these rules, and one draw needn't show every extreme that they name: `keep`: within every aligned block of 64 positions of a request, between 16 and 31 entries are 1, and some block has exactly 31. `lengths`: multiples of 64; the first request of every 8 in order has 8192. `route`: A permutation of the requests. `log_forget`: Negative.
All inputs are finite; a program needn't handle non-finite values.
Results may differ from a plain program's by a relative error of at most 0.0085.
Values may be sent and summed in bfloat16 or wider, within the bound.
A program may use at most 64 MiB of HBM per device.

v0:
```python
import jax
import jax.numpy as jnp
from jax import lax
from jax.sharding import PartitionSpec as P

BLOCK = 64
SLOTS = 32
EMPTY_LOG = -10000.0
HIGHEST = lax.Precision.HIGHEST


def shards(
    keys, values, log_forget, keep, merge_weight, lengths, route, fresh, new_forget, out_weight
):
    f32, bf16 = (jnp.float32, jnp.bfloat16)
    req_dev, pos_dev, width_dev = keys.shape
    heads_dev = log_forget.shape[1]
    head_size = width_dev // heads_dev
    blocks_dev = pos_dev // BLOCK
    rows_dev = blocks_dev * SLOTS
    n_seq = lax.axis_size("seq")
    shard = lax.axis_index("seq")
    grp_req = fresh.shape[1]
    packed_fresh = jnp.concatenate(
        [fresh.transpose(1, 0, 2).reshape(grp_req, 3 * width_dev), new_forget], axis=1
    )
    arrived = lax.all_gather(packed_fresh, "grp", axis=0, tiled=True)
    picked = jnp.take(arrived, route, axis=0)
    query = picked[:, :width_dev]
    own_key = picked[:, width_dev : 2 * width_dev]
    own_value = picked[:, 2 * width_dev : 3 * width_dev].astype(f32)
    new_log = picked[:, 3 * width_dev :].astype(f32)
    position = shard * pos_dev + jnp.arange(pos_dev, dtype=jnp.int32)
    live = position[None, :] < lengths[:, None]
    forget = jnp.where(live[:, None, :], log_forget, 0.0)
    forget_blocks = forget.reshape(req_dev, heads_dev, blocks_dev, BLOCK)
    at = jnp.arange(BLOCK, dtype=jnp.int32)
    after = (at[:, None] > at[None, :]).astype(f32)
    within = jnp.einsum("rhbt,tp->rhbp", forget_blocks, after, precision=HIGHEST)
    block_total = jnp.sum(forget_blocks, axis=3)
    own_total = jnp.sum(block_total, axis=2)
    bt = jnp.arange(blocks_dev, dtype=jnp.int32)
    later_block = jnp.einsum(
        "rhb,bc->rhc", block_total, (bt[:, None] > bt[None, :]).astype(f32), precision=HIGHEST
    )
    totals = lax.all_gather(own_total, "seq")
    later_shard = jnp.sum(
        jnp.where((jnp.arange(n_seq) > shard)[:, None, None], totals, 0.0), axis=0
    )
    decay_blocks = within + later_block[..., None] + later_shard[:, :, None, None]
    flags = keep.reshape(req_dev, blocks_dev, BLOCK)
    upto = (at[:, None] <= at[None, :]).astype(bf16)
    rank = (
        jnp.einsum("rbt,tp->rbp", flags.astype(bf16), upto, preferred_element_type=f32).astype(
            jnp.int32
        )
        - 1
    )
    slot_ids = jnp.arange(SLOTS - 1, dtype=jnp.int32)
    block_start = shard * pos_dev + bt * BLOCK
    block_live = (block_start[None, :] < lengths[:, None]).astype(f32)
    chosen = (
        (flags[:, :, None, :] == 1) & (rank[:, :, None, :] == slot_ids[None, None, :, None])
    ).astype(f32)
    chosen = chosen * block_live[:, :, None, None]
    dropped = flags == 0
    weighted = jnp.where(dropped, merge_weight.reshape(req_dev, blocks_dev, BLOCK), 0.0)
    share = (weighted / jnp.sum(weighted, axis=2, keepdims=True)).astype(bf16).astype(f32)
    merged_row = (share * block_live[:, :, None])[:, :, None, :]
    select = jnp.concatenate([chosen, merged_row], axis=2).astype(bf16)
    key_blocks = keys.reshape(req_dev, blocks_dev, BLOCK, width_dev)
    value_blocks = values.reshape(req_dev, blocks_dev, BLOCK, width_dev)
    packed_keys = (
        jnp.einsum("rbej,rbjc->rbec", select, key_blocks, preferred_element_type=f32)
        .astype(bf16)
        .reshape(req_dev, rows_dev, width_dev)
    )
    packed_values = (
        jnp.einsum("rbej,rbjc->rbec", select, value_blocks, preferred_element_type=f32)
        .astype(bf16)
        .reshape(req_dev, rows_dev, width_dev)
    )
    dealt = lax.all_to_all(
        jnp.stack([packed_keys, packed_values]), "seq", split_axis=2, concat_axis=2, tiled=True
    )
    kept_log = jnp.einsum("rbej,rhbj->rhbe", chosen, decay_blocks, precision=HIGHEST)
    filled = jnp.sum(chosen, axis=3)
    kept_log = kept_log + (1.0 - filled)[:, None, :, :] * EMPTY_LOG
    drop_mask = dropped[:, None, :, :]
    drop_peak = jnp.max(jnp.where(drop_mask, decay_blocks, -jnp.inf), axis=3)
    spread = jnp.where(drop_mask, jnp.exp(decay_blocks - drop_peak[..., None]), 0.0)
    merged_log = drop_peak + jnp.log(jnp.sum(share[:, None, :, :] * spread, axis=3))
    merged_log = jnp.where(block_live[:, None, :] > 0, merged_log, EMPTY_LOG)
    slot_log = jnp.concatenate([kept_log, merged_log[..., None]], axis=3).reshape(
        req_dev, heads_dev, rows_dev
    )
    compact_decay = jnp.exp(slot_log)
    scale = head_size ** (-0.5)
    head_of = jnp.arange(width_dev, dtype=jnp.int32) // head_size
    onehot = head_of[:, None] == jnp.arange(heads_dev, dtype=jnp.int32)[None, :]
    query_blocks = jnp.where(onehot[None], query[:, :, None], jnp.zeros((), bf16))
    scores = (
        jnp.einsum("rnc,rch->rhn", packed_keys, query_blocks, preferred_element_type=f32) * scale
        + slot_log
    )
    local_top = jnp.max(scores, axis=2)
    weights = jnp.exp(scores - local_top[..., None]).astype(bf16)
    local_sum = jnp.sum(weights.astype(f32), axis=2)
    full_acc = jnp.einsum("rhn,rnc->rhc", weights, packed_values, preferred_element_type=f32)
    local_acc = jnp.sum(jnp.where(onehot.T[None], full_acc, 0.0), axis=1)
    stats = jnp.concatenate([local_top, local_sum, local_acc], axis=1)
    every = lax.all_gather(stats, "seq")
    tops = every[:, :, :heads_dev]
    sums = every[:, :, heads_dev : 2 * heads_dev]
    accs = every[:, :, 2 * heads_dev :]
    top = jnp.max(tops, axis=0)
    rescale = jnp.exp(tops - top[None])
    total_sum = jnp.sum(rescale * sums, axis=0)
    total_acc = jnp.sum(jnp.repeat(rescale, head_size, axis=2) * accs, axis=0)
    own_score = (
        jnp.sum(
            (query.astype(f32) * own_key.astype(f32)).reshape(req_dev, heads_dev, head_size), axis=2
        )
        * scale
    )
    cache_top = top + new_log
    joint = jnp.maximum(cache_top, own_score)
    cache_scale = jnp.exp(cache_top - joint)
    self_weight = jnp.exp(own_score - joint)
    numer = (
        jnp.repeat(cache_scale, head_size, axis=1) * total_acc
        + jnp.repeat(self_weight, head_size, axis=1) * own_value
    )
    denom = jnp.repeat(cache_scale * total_sum + self_weight, head_size, axis=1)
    attended = (numer / denom).astype(bf16)
    partial_out = jnp.dot(attended, out_weight, preferred_element_type=f32)
    layer_out = lax.psum(partial_out, "head").astype(bf16)
    return (dealt[0], dealt[1], compact_decay, layer_out)


def solution(mesh):
    return jax.shard_map(
        shards,
        mesh=mesh,
        in_specs=(
            P("grp", "seq", "head"),
            P("grp", "seq", "head"),
            P("grp", "head", "seq"),
            P("grp", "seq"),
            P("grp", "seq"),
            P("grp"),
            P("grp"),
            P(None, "grp", "head"),
            P("grp", "head"),
            P("head", "seq"),
        ),
        out_specs=(
            P("grp", "seq", "head"),
            P("grp", "seq", "head"),
            P("grp", "head", "seq"),
            P("grp", "seq"),
        ),
        check_vma=False,
    )
```

profile of v0, /device:TPU:16, one launch (start us, length us, event | category | flops | bytes accessed | tf_op | source)
XLA Modules:
  0.0 155.7 jit_solution(16878182813551151916)
XLA Ops:
  0.6 0.9 broadcast_compare_fusion.2
  1.5 0.8 convert_element_type.92
  2.3 0.7 broadcast_select_fusion.4
  3.1 0.8 reshape.315
  4.3 1.3 broadcast_compare_fusion.3
  6.2 0.7 convolution_convert_fusion
  7.0 1.7 %copy-done.4 = bf16[8,512,384]{2,1,0:T(8,128)(2,1)S(1)} copy-done((bf16[8,512,384]{2,1,0:T(8,128)(2,1)S(1)}, bf16[8,512,384]{2,1,0:T(8,128)(2,1)}, u32[]{:S(2)}) %copy-start.4) | copy-done | bytes 3145752
  9.3 0.9 copy.48
  10.4 0.9 copy.49
  11.4 2.1 %pad_maximum_fusion = bf16[2,8,256,384]{3,1,0,2:T(8,128)(2,1)} fusion(bf16[1,8,256,384]{3,1,0,2:T(8,128)(2,1)S(1)} %copy.49, bf16[1,8,256,384]{3,1,0,2:T(8,128)(2,1)S(1)} %copy.48), kind=kLoop, calls=%fused_computation.1 | loop fusion | flops 1572864 | bytes 6291456 | tf_op jit(solution)/shard_map/stack | solution.py:84
  13.5 8.8 %all-to-all-start = ((bf16[2,8,256,384]{3,1,0,2:T(8,128)(2,1)}), bf16[2,8,256,384]{3,1,0,2:T(8,128)(2,1)}, u32[]{:S(2)}, u32[]{:S(2)}) async-start(bf16[2,8,256,384]{3,1,0,2:T(8,128)(2,1)} %pad_maximum_fusion), calls=%async_computation | async-start | bytes 6291456 | tf_op jit(solution)/shard_map/all_to_all | solution.py:83
  22.3 10.7 %all_gather.17 = bf16[32,1158]{1,0:T(8,128)(2,1)S(1)} all-gather(bf16[8,1158]{1,0:T(8,128)(2,1)S(1)} %pad_maximum_fusion.5), channel_id=1, replica_groups=mesh['grp'=4,'seq'=16,'head'=4] {'grp'}, dimensions={0}, use_global_device_ids=true | all-gather | bytes 92640 | tf_op jit(solution)/shard_map/all_gather | solution.py:27
  34.6 69.8 %all-gather = f32[128,6]{1,0:T(8,128)S(1)} all-gather(f32[8,6]{1,0:T(8,128)S(1)} %copy.52), channel_id=2, replica_groups=mesh['grp'=4,'seq'=16,'head'=4] {'seq'}, dimensions={0}, use_global_device_ids=true | all-gather | bytes 3264 | tf_op jit(solution)/shard_map/all_gather | solution.py:46
  104.7 0.7 copy.54
  105.5 0.7 reduce_sum.107
  106.4 0.8 fusion.33
  107.2 1.0 select_reduce_fusion.1
  110.1 2.8 %fusion.5 = f32[8,6,8,31]{3,1,2,0:T(8,128)S(1)} fusion(f32[8,8]{1,0:T(8,128)S(1)} %copy-done.10, s32[8,8,64]{2,1,0:T(8,128)S(1)} %fusion.12, pred[8,8,64]{2,1,0:T(8,128)(4,1)S(1)} %eq.81, f32[8,6,8,64]{3,2,1,0:T(8,128)} %copy-done.5, f32[8,8,31]{2,1,0:T(8,128)S(1)} %subtract_multiply_fusion), kind=kOutput, calls=%fused_computation.11 | convolution fusion | flops 9535104 | bytes 174592 | tf_op jit(solution)/shard_map/rbej,rhbj->rhbe/dot_general | solution.py:86
  113.9 2.0 %fusion.51 = (f32[8,6]{1,0:T(8,128)S(1)}, f32[8,6,256]{2,1,0:T(8,128)S(1)}) fusion(f32[8,6,256]{2,0,1:T(8,128)S(1)} %reshape.319, bf16[8,256,384]{2,1,0:T(8,128)(2,1)} %bitcast.50, pred[384,6]{0,1:T(8,128)(4,1)S(1)} %iota_compare_fusion.4, bf16[8,384]{1,0:T(8,128)(2,1)S(1)} %copy-done.12), kind=kOutput, calls=%fused_computation.102 | convolution fusion | flops 9492432 | bytes 1679808 | tf_op jit(solution)/shard_map/rnc,rch->rhn/dot_general | solution.py:103
  116.6 15.4 %all-gather.1 = f32[128,396]{1,0:T(8,128)S(1)} all-gather(f32[8,396]{1,0:T(8,128)S(1)} %pad_maximum_fusion.6), channel_id=3, replica_groups=mesh['grp'=4,'seq'=16,'head'=4] {'seq'}, dimensions={0}, use_global_device_ids=true | all-gather | bytes 215424 | tf_op jit(solution)/shard_map/all_gather | solution.py:112
  132.1 0.7 multiply_add_fusion
  132.8 0.7 reshape.327
  133.6 0.7 reshape.324
  134.3 0.7 reshape.326
  135.0 1.0 broadcast_in_dim.169
  136.0 1.9 %reshape.325 = f32[16,8,384]{2,1,0:T(8,128)} reshape(f32[16,8,6,64]{3,2,1,0:T(8,128)} %broadcast_in_dim.169) | data formatting | bytes 393216 | tf_op jit(solution)/shard_map/reshape | solution.py:119
  137.9 1.0 fusion.20
  138.9 0.9 fusion.35
  139.8 11.1 %psum.7 = bf16[8,96]{1,0:T(8,128)(2,1)} all-reduce(f32[8,96]{1,0:T(8,128)S(1)} %fusion.35), channel_id=1, replica_groups=mesh['grp'=4,'seq'=16,'head'=4] {'head'}, use_global_device_ids=true, to_apply=%region_14.15 | all-reduce | flops 768 | bytes 4608 | tf_op jit(solution)/shard_map/psum | solution.py:137
  150.9 2.2 %slice_bitcast_fusion = (bf16[8,256,384]{2,0,1:T(8,128)(2,1)S(1)}, bf16[8,256,384]{2,0,1:T(8,128)(2,1)S(1)}) fusion(bf16[2,8,256,384]{3,1,0,2:T(8,128)(2,1)} %all-to-all-done), kind=kLoop, calls=%fused_computation.8 | loop fusion | bytes 6291456 | tf_op jit(solution)/shard_map/squeeze | solution.py:138
  153.1 1.3 copy.61
  154.4 1.3 copy.60
  (88 shorter events, 8.0 us)
Async XLA Ops:
  0.6 5.6 %copy-start = (bf16[8,512,384]{2,1,0:T(8,128)(2,1)S(1)}, bf16[8,512,384]{2,1,0:T(8,128)(2,1)}, u32[]{:S(2)}) copy-start(bf16[8,512,384]{2,1,0:T(8,128)(2,1)} %param.11) | copy-start | bytes 9437188
  5.6 1.3 copy-start.9
  5.7 1.2 copy-start.11
  6.2 2.4 %copy-start.4 = (bf16[8,512,384]{2,1,0:T(8,128)(2,1)S(1)}, bf16[8,512,384]{2,1,0:T(8,128)(2,1)}, u32[]{:S(2)}) copy-start(bf16[8,512,384]{2,1,0:T(8,128)(2,1)} %param.10) | copy-start | bytes 9437188
  7.0 3.5 %copy-start.1 = (bf16[8,8,32,384]{3,2,1,0:T(8,128)(2,1)}, bf16[8,8,32,384]{3,2,1,0:T(8,128)(2,1)S(1)}, u32[]{:S(2)}) copy-start(bf16[8,8,32,384]{3,2,1,0:T(8,128)(2,1)S(1)} %convolution_convert_fusion) | copy-start | bytes 4718596
  9.3 1.1 copy-start.3
  13.5 8.8 %copy-start.18 = (s32[8]{0:T(128)S(1)}, s32[8]{0:T(128)}, u32[]{:S(2)}) copy-start(s32[8]{0:T(128)} %param.16) | copy-start | bytes 100
  13.5 8.8 %copy-start.13 = (bf16[3,8,384]{2,1,0:T(8,128)(2,1)S(1)}, bf16[3,8,384]{2,1,0:T(8,128)(2,1)}, u32[]{:S(2)}) copy-start(bf16[3,8,384]{2,1,0:T(8,128)(2,1)} %param.17) | copy-start | bytes 55300
  13.5 8.8 %copy-start.16 = (bf16[8,6]{1,0:T(8,128)(2,1)S(1)}, bf16[8,6]{1,0:T(8,128)(2,1)}, u32[]{:S(2)}) copy-start(bf16[8,6]{1,0:T(8,128)(2,1)} %param.18) | copy-start | bytes 292
  13.5 20.9 %copy-start.17 = (s32[8]{0:T(128)S(1)}, s32[8]{0:T(128)}, u32[]{:S(2)}) copy-start(s32[8]{0:T(128)} %param.15) | copy-start | bytes 100
  13.5 21.0 %copy-start.7 = (f32[8,6,512]{2,0,1:T(8,128)S(1)}, f32[8,6,512]{2,0,1:T(8,128)}, u32[]{:S(2)}) copy-start(f32[8,6,512]{2,0,1:T(8,128)} %param.12) | copy-start | bytes 294916
  13.5 137.3 %all-to-all-start = ((bf16[2,8,256,384]{3,1,0,2:T(8,128)(2,1)}), bf16[2,8,256,384]{3,1,0,2:T(8,128)(2,1)}, u32[]{:S(2)}, u32[]{:S(2)}) async-start(bf16[2,8,256,384]{3,1,0,2:T(8,128)(2,1)} %pad_maximum_fusion), calls=%async_computation | async-start | bytes 6291456 | tf_op jit(solution)/shard_map/all_to_all | solution.py:83
  33.7 0.6 copy-start.6
  106.1 3.2 %copy-start.10 = (f32[8,8]{1,0:T(8,128)S(1)}, f32[8,8]{1,0:T(8,128)}, u32[]{:S(2)}) copy-start(f32[8,8]{1,0:T(8,128)} %copy-done.9) | copy-start | bytes 772
  106.1 3.8 %copy-start.15 = (pred[8,8]{1,0:T(8,128)(4,1)S(1)}, pred[8,8]{1,0:T(8,128)(4,1)}, u32[]{:S(2)}) copy-start(pred[8,8]{1,0:T(8,128)(4,1)} %get-tuple-element.31) | copy-start | bytes 196
  108.2 0.7 copy-start.5
  110.0 4.0 %copy-start.12 = (bf16[8,384]{1,0:T(8,128)(2,1)S(1)}, bf16[8,384]{1,0:T(8,128)(2,1)}, u32[]{:S(2)}) copy-start(bf16[8,384]{1,0:T(8,128)(2,1)} %slice.40) | copy-start | bytes 18436
  113.2 2.9 %copy-start.2 = (bf16[8,8,32,384]{3,2,1,0:T(8,128)(2,1)S(1)}, bf16[8,8,32,384]{3,2,1,0:T(8,128)(2,1)}, u32[]{:S(2)}) copy-start(bf16[8,8,32,384]{3,2,1,0:T(8,128)(2,1)} %copy-done.1) | copy-start | bytes 4718596
  115.9 16.2 %copy-start.14 = (f32[8,6]{1,0:T(8,128)S(1)}, f32[8,6]{1,0:T(8,128)}, u32[]{:S(2)}) copy-start(f32[8,6]{1,0:T(8,128)} %reduce_sum.107) | copy-start | bytes 580
  135.0 3.9 %copy-start.8 = (bf16[384,96]{0,1:T(8,128)(2,1)S(1)}, bf16[384,96]{0,1:T(8,128)(2,1)}, u32[]{:S(2)}) copy-start(bf16[384,96]{0,1:T(8,128)(2,1)} %param.19) | copy-start | bytes 221188
where the time goes:
time: 157 us; the launch traced here: 156 us
  blocking collectives  107 us (68%)
  local copies, waits for them, and re-layouts  18.8 us (12%)
  other arithmetic  11.5 us (7%)
  starting transfers between devices  8.76 us (6%)
  matrix products  8.72 us (6%)
    all_gather x1, blocking collectives, shards(): totals = lax.all_gather(own_total, 'seq')  69.8 us
    all_gather x1, blocking collectives, shards(): every = lax.all_gather(stats, 'seq')  15.4 us
    psum x1, blocking collectives, shards(): layer_out = lax.psum(partial_out, 'head').astype(bf16)  11.1 us
    all_gather x1, blocking collectives, shards(): arrived = lax.all_gather(packed_fresh, 'grp', axis=0, tiled=True)  10.7 us
    all_to_all x1, starting transfers between devices, shards(): lax.all_to_all(jnp.stack([packed_keys, packed_values]), 'seq', split_axis...  8.76 us
    unnamed x40, local copies, waits for them, and re-layouts  5.05 us
  transfers between devices with their start and end apart: 1, of which 0 were waited for; matrix products, arithmetic and copies ran while one was open for 13% of the time, Pallas kernels for 0%

commit v1 on v0

--- a/solution.py
+++ b/solution.py
@@ -1,12 +1,44 @@
+import functools
 import jax
 import jax.numpy as jnp
 from jax import lax
 from jax.sharding import PartitionSpec as P
+from jax.lax import axis_index, axis_size, ppermute
 
 BLOCK = 64
 SLOTS = 32
 EMPTY_LOG = -10000.0
 HIGHEST = lax.Precision.HIGHEST
+
+
+def streams_place(field_in, dim_k):
+    low = axis_size("grp")
+    shaped = axis_index("grp")
+    upper, r1, newest = (low, shaped, field_in.shape[dim_k])
+    bank = [ix * upper if dev_i == dim_k else ix for dev_i, ix in enumerate(field_in.shape)]
+    w2 = jnp.zeros(bank, field_in.dtype)
+    part_now = lax.dynamic_update_slice_in_dim(w2, field_in, r1 * newest, axis=dim_k)
+    mid_arr = met_up = field_in
+    for kk in tuple(range(1, upper // 2 + 1)):
+        mid_arr = ppermute(
+            mid_arr, axis_name="grp", perm=[(dev_i, (dev_i + 1) % upper) for dev_i in range(upper)]
+        )
+        part_now = lax.dynamic_update_slice_in_dim(
+            part_now, mid_arr, (r1 - kk) % upper * newest, axis=dim_k
+        )
+        if 2 * kk < upper:
+            met_up = ppermute(
+                met_up,
+                axis_name="grp",
+                perm=[(dev_i, (dev_i - 1) % upper) for dev_i in range(upper)],
+            )
+            part_now = lax.dynamic_update_slice_in_dim(
+                part_now, met_up, (r1 + kk) % upper * newest, axis=dim_k
+            )
+    return part_now
+
+
+pack_plate = functools.partial(streams_place, dim_k=0)
 
 
 def shards(
@@ -24,7 +56,7 @@
     packed_fresh = jnp.concatenate(
         [fresh.transpose(1, 0, 2).reshape(grp_req, 3 * width_dev), new_forget], axis=1
     )
-    arrived = lax.all_gather(packed_fresh, "grp", axis=0, tiled=True)
+    arrived = pack_plate(packed_fresh)
     picked = jnp.take(arrived, route, axis=0)
     query = picked[:, :width_dev]
     own_key = picked[:, width_dev : 2 * width_dev]

time: 157 us -> 167 us (1.064); the launches traced: 156 us -> 164 us
  starting transfers between devices: 8.76 us -> 12.1 us
  other arithmetic: 11.5 us -> 13.4 us
    all_gather x1, blocking collectives: 69.8 us -> 81.2 us  [shards(): totals = lax.all_gather(own_total, 'seq')]
    all_gather x1 -> x0, blocking collectives: 10.7 us -> none  [shards(): arrived = lax.all_gather(packed_fresh, 'grp', axis=0, tiled=True)]
    ppermute x0 -> x3, starting transfers between devices: none -> 3.31 us  [the longest x2 2.57 us: streams_place(): ppermute(mid_arr, axis_name='grp', perm=[(dev_i, (dev_i + 1) % upper) for...]
    unnamed x40 -> x28, local copies, waits for them, and re-layouts: 5.05 us -> 4.61 us
  transfers between devices with their start and end apart: 1 -> 4, of which waited for: 0 -> 1; matrix products, arithmetic and copies ran while one was open for 13% -> 20% of each run, Pallas kernels for 0% -> 0%
where the time goes in v1:
time: 167 us; the launch traced here: 164 us
  blocking collectives  108 us (65%)
  local copies, waits for them, and re-layouts  20 us (12%)
  other arithmetic  13.4 us (8%)
  starting transfers between devices  12.1 us (7%)
  matrix products  8.31 us (5%)
    all_gather x1, blocking collectives, shards(): totals = lax.all_gather(own_total, 'seq')  81.2 us
    all_gather x1, blocking collectives, shards(): every = lax.all_gather(stats, 'seq')  15.4 us
    psum x1, blocking collectives, shards(): layer_out = lax.psum(partial_out, 'head').astype(bf16)  11 us
    all_to_all x1, starting transfers between devices, shards(): lax.all_to_all(jnp.stack([packed_keys, packed_values]), 'seq', split_axis...  8.75 us
    unnamed x28, local copies, waits for them, and re-layouts  4.61 us
  transfers between devices with their start and end apart: 4, of which 1 were waited for; matrix products, arithmetic and copies ran while one was open for 20% of the time, Pallas kernels for 0%

profile of v1, /device:TPU:16, one launch (start us, length us, event | category | flops | bytes accessed | tf_op | source)
XLA Modules:
  0.0 163.7 jit_solution(9602401355627101972)
XLA Ops:
  0.7 1.5 pad_maximum_fusion.5
  2.2 1.3 collective-permute-start
  3.5 0.7 collective-permute-start.1
  5.6 0.7 broadcast_select_fusion.4
  6.4 0.8 reshape.315
  7.7 1.3 broadcast_compare_fusion.3
  10.3 1.7 %copy-done.4 = bf16[8,512,384]{2,1,0:T(8,128)(2,1)S(1)} copy-done((bf16[8,512,384]{2,1,0:T(8,128)(2,1)S(1)}, bf16[8,512,384]{2,1,0:T(8,128)(2,1)}, u32[]{:S(2)}) %copy-start.4) | copy-done | bytes 3145752
  12.6 0.9 copy.48
  13.8 0.9 copy.49
  14.7 2.1 %pad_maximum_fusion = bf16[2,8,256,384]{3,1,0,2:T(8,128)(2,1)} fusion(bf16[1,8,256,384]{3,1,0,2:T(8,128)(2,1)S(1)} %copy.49, bf16[1,8,256,384]{3,1,0,2:T(8,128)(2,1)S(1)} %copy.48), kind=kLoop, calls=%fused_computation.1 | loop fusion | flops 1572864 | bytes 6291456 | tf_op jit(solution)/shard_map/stack | solution.py:116
  16.8 8.7 %all-to-all-start = ((bf16[2,8,256,384]{3,1,0,2:T(8,128)(2,1)}), bf16[2,8,256,384]{3,1,0,2:T(8,128)(2,1)}, u32[]{:S(2)}, u32[]{:S(2)}) async-start(bf16[2,8,256,384]{3,1,0,2:T(8,128)(2,1)} %pad_maximum_fusion), calls=%async_computation | async-start | bytes 6291456 | tf_op jit(solution)/shard_map/all_to_all | solution.py:115
  26.5 81.2 %all-gather = f32[128,6]{1,0:T(8,128)S(1)} all-gather(f32[8,6]{1,0:T(8,128)S(1)} %copy.52), channel_id=2, replica_groups=mesh['grp'=4,'seq'=16,'head'=4] {'seq'}, dimensions={0}, use_global_device_ids=true | all-gather | bytes 3264 | tf_op jit(solution)/shard_map/all_gather | solution.py:78
  108.1 1.0 reshape.318
  109.7 1.0 multiply_reduce_fusion
  111.1 1.2 select_reduce_fusion
  112.3 0.8 broadcast_select_fusion
  113.1 2.8 %fusion.5 = f32[8,6,8,31]{3,1,2,0:T(8,128)S(1)} fusion(f32[8,8]{1,0:T(8,128)} %copy-done.9, s32[8,8,64]{2,1,0:T(8,128)S(1)} %fusion.12, pred[8,8,64]{2,1,0:T(8,128)(4,1)} %copy-done.8, f32[8,6,8,64]{3,2,1,0:T(8,128)} %copy-done.5, f32[8,8,31]{2,1,0:T(8,128)S(1)} %subtract_multiply_fusion), kind=kOutput, calls=%fused_computation.11 | convolution fusion | flops 9535104 | bytes 174592 | tf_op jit(solution)/shard_map/rbej,rhbj->rhbe/dot_general | solution.py:118
  117.0 1.0 reshape.319
  118.6 1.3 collective-permute-start.2
  119.9 0.8 constant_dynamic-update-slice_fusion.2
  120.7 0.7 constant_dynamic-update-slice_fusion.1
  121.4 1.2 collective-permute-done.2
  123.5 2.1 %fusion.51 = (f32[8,6]{1,0:T(8,128)S(1)}, f32[8,6,256]{2,1,0:T(8,128)S(1)}) fusion(f32[8,6,256]{2,0,1:T(8,128)S(1)} %reshape.319, bf16[8,256,384]{2,1,0:T(8,128)(2,1)} %bitcast.50, pred[384,6]{0,1:T(8,128)(4,1)S(1)} %iota_compare_fusion.4, bf16[8,384]{1,0:T(8,128)(2,1)S(1)} %slice.40), kind=kOutput, calls=%fused_computation.106 | convolution fusion | flops 9492432 | bytes 1679808 | tf_op jit(solution)/shard_map/rnc,rch->rhn/dot_general | solution.py:135
  126.2 15.4 %all-gather.1 = f32[128,396]{1,0:T(8,128)S(1)} all-gather(f32[8,396]{1,0:T(8,128)S(1)} %pad_maximum_fusion.6), channel_id=3, replica_groups=mesh['grp'=4,'seq'=16,'head'=4] {'seq'}, dimensions={0}, use_global_device_ids=true | all-gather | bytes 215424 | tf_op jit(solution)/shard_map/all_gather | solution.py:144
  142.8 1.0 broadcast_in_dim.173
  143.8 1.9 %reshape.325 = f32[16,8,384]{2,1,0:T(8,128)} reshape(f32[16,8,6,64]{3,2,1,0:T(8,128)} %broadcast_in_dim.173) | data formatting | bytes 393216 | tf_op jit(solution)/shard_map/reshape | solution.py:151
  145.6 1.0 fusion.20
  146.7 1.0 fusion.35
  147.7 11.0 %psum.7 = bf16[8,96]{1,0:T(8,128)(2,1)} all-reduce(f32[8,96]{1,0:T(8,128)S(1)} %fusion.35), channel_id=1, replica_groups=mesh['grp'=4,'seq'=16,'head'=4] {'head'}, use_global_device_ids=true, to_apply=%region_14.15 | all-reduce | flops 768 | bytes 4608 | tf_op jit(solution)/shard_map/psum | solution.py:169
  158.8 2.2 %slice_bitcast_fusion = (bf16[8,256,384]{2,0,1:T(8,128)(2,1)S(1)}, bf16[8,256,384]{2,0,1:T(8,128)(2,1)S(1)}) fusion(bf16[2,8,256,384]{3,1,0,2:T(8,128)(2,1)} %all-to-all-done), kind=kLoop, calls=%fused_computation.8 | loop fusion | bytes 6291456 | tf_op jit(solution)/shard_map/squeeze | solution.py:170
  161.0 1.3 copy.61
  162.3 1.3 copy.60
  (85 shorter events, 10.6 us)
Async XLA Ops:
  0.6 8.9 %copy-start = (bf16[8,512,384]{2,1,0:T(8,128)(2,1)S(1)}, bf16[8,512,384]{2,1,0:T(8,128)(2,1)}, u32[]{:S(2)}) copy-start(bf16[8,512,384]{2,1,0:T(8,128)(2,1)} %param.11) | copy-start | bytes 9437188
  2.2 116.5 %collective-permute-start = (bf16[8,1158]{1,0:T(8,128)(2,1)}, bf16[8,1158]{1,0:T(8,128)(2,1)}, u32[]{:S(2)}, u32[]{:S(2)}) collective-permute-start(bf16[8,1158]{1,0:T(8,128)(2,1)} %get-tuple-element.31), channel_id=1, source_target_pairs={{0,64},{64,128},{128,192},{192,0},{1,65},{65,129},{129,193},{193,1... | collective-permute-start | bytes 55592 | tf_op jit(solution)/shard_map/ppermute | solution.py:23
  3.5 117.2 %collective-permute-start.1 = (bf16[8,1158]{1,0:T(8,128)(2,1)}, bf16[8,1158]{1,0:T(8,128)(2,1)}, u32[]{:S(2)}, u32[]{:S(2)}) collective-permute-start(bf16[8,1158]{1,0:T(8,128)(2,1)} %get-tuple-element.31), channel_id=1, source_target_pairs={{0,192},{64,0},{128,64},{192,128},{1,193},{65,1},{129,65},{193,129... | collective-permute-start | bytes 55592 | tf_op jit(solution)/shard_map/ppermute | solution.py:30
  7.3 3.0 %copy-start.8 = (pred[8,8,64]{2,1,0:T(8,128)(4,1)}, pred[8,8,64]{2,1,0:T(8,128)(4,1)S(1)}, u32[]{:S(2)}) copy-start(pred[8,8,64]{2,1,0:T(8,128)(4,1)S(1)} %eq.85) | copy-start | bytes 12292
  7.6 101.8 %copy-start.6 = (pred[8,8,64]{2,1,0:T(8,128)(4,1)}, pred[8,8,64]{2,1,0:T(8,128)(4,1)S(1)}, u32[]{:S(2)}) copy-start(pred[8,8,64]{2,1,0:T(8,128)(4,1)S(1)} %eq.91) | copy-start | bytes 12292
  9.0 1.3 copy-start.9
  9.6 2.4 %copy-start.4 = (bf16[8,512,384]{2,1,0:T(8,128)(2,1)S(1)}, bf16[8,512,384]{2,1,0:T(8,128)(2,1)}, u32[]{:S(2)}) copy-start(bf16[8,512,384]{2,1,0:T(8,128)(2,1)} %param.10) | copy-start | bytes 9437188
  10.3 3.5 %copy-start.1 = (bf16[8,8,32,384]{3,2,1,0:T(8,128)(2,1)}, bf16[8,8,32,384]{3,2,1,0:T(8,128)(2,1)S(1)}, u32[]{:S(2)}) copy-start(bf16[8,8,32,384]{3,2,1,0:T(8,128)(2,1)S(1)} %convolution_convert_fusion) | copy-start | bytes 4718596
  12.6 1.1 copy-start.3
  16.8 8.9 %copy-start.11 = (s32[8]{0:T(128)S(1)}, s32[8]{0:T(128)}, u32[]{:S(2)}) copy-start(s32[8]{0:T(128)} %param.15) | copy-start | bytes 100
  16.8 9.0 %copy-start.7 = (f32[8,6,512]{2,0,1:T(8,128)S(1)}, f32[8,6,512]{2,0,1:T(8,128)}, u32[]{:S(2)}) copy-start(f32[8,6,512]{2,0,1:T(8,128)} %param.12) | copy-start | bytes 294916
  16.8 141.9 %all-to-all-start = ((bf16[2,8,256,384]{3,1,0,2:T(8,128)(2,1)}), bf16[2,8,256,384]{3,1,0,2:T(8,128)(2,1)}, u32[]{:S(2)}, u32[]{:S(2)}) async-start(bf16[2,8,256,384]{3,1,0,2:T(8,128)(2,1)} %pad_maximum_fusion), calls=%async_computation | async-start | bytes 6291456 | tf_op jit(solution)/shard_map/all_to_all | solution.py:115
  109.7 1.0 copy-start.5
  111.1 5.0 %copy-start.12 = (s32[8]{0:T(128)S(1)}, s32[8]{0:T(128)}, u32[]{:S(2)}) copy-start(s32[8]{0:T(128)} %param.16) | copy-start | bytes 100
  118.6 4.0 %collective-permute-start.2 = (bf16[8,1158]{1,0:T(8,128)(2,1)}, bf16[8,1158]{1,0:T(8,128)(2,1)S(1)}, u32[]{:S(2)}, u32[]{:S(2)}) collective-permute-start(bf16[8,1158]{1,0:T(8,128)(2,1)} %collective-permute-done), channel_id=1, source_target_pairs={{0,64},{64,128},{128,192},{192,0},{1,65},{65,129},{129,193},{193,1... | collective-permute-start | bytes 55592 | tf_op jit(solution)/shard_map/ppermute | solution.py:23
  123.5 2.3 %copy-start.2 = (bf16[8,8,32,384]{3,2,1,0:T(8,128)(2,1)S(1)}, bf16[8,8,32,384]{3,2,1,0:T(8,128)(2,1)}, u32[]{:S(2)}) copy-start(bf16[8,8,32,384]{3,2,1,0:T(8,128)(2,1)} %copy-done.1) | copy-start | bytes 4718596
  142.8 3.9 %copy-start.10 = (f32[8,384]{1,0:T(8,128)S(1)}, f32[8,384]{1,0:T(8,128)}, u32[]{:S(2)}) copy-start(f32[8,384]{1,0:T(8,128)} %reshape.326) | copy-start | bytes 36868
